TPU v7x, 32 devices: a whole 2x2x4 slice. The times are simulated.
32 devices in a mesh: rows: 4 (over y, x), cols: 8 (over z, core).
Axes of the slice: x: 2, y: 2, z: 4, core: 2. Of those that a mesh axis runs over, the one named last changes fastest.
Arguments:
- images: bfloat16 [2, 64, 256, 1024], P(None, None, 'rows', 'cols'), may hold values from -6 to 6
- first_weight: bfloat16 [9, 64, 64], replicated, may hold values from -0.25 to 0.25
- second_weight: bfloat16 [9, 64, 64], replicated, may hold values from -0.25 to 0.25
- search_ranges: int32 [2, 32, 8], P(None, 'rows', 'cols'), may hold values from 0 to 16, as said below
Outputs:
- matched: bfloat16 [64, 256, 1024], P(None, 'rows', 'cols')
- disparity: float32 [256, 1024], P('rows', 'cols')
Inputs may be any that keep to these rules, and one draw needn't show every extreme that they name: search_ranges[0] is 0 to 1 and search_ranges[1] is 1 to 16; some block has search_ranges[0] = 1 together with search_ranges[1] = 16.
All inputs are finite; a program needn't handle non-finite values.
Results may differ from a plain program's by a relative error of at most 0.008.
Values may be sent and summed in bfloat16 or wider, within the bound.
No kernel may reach another device: no remote copies, remote signals or barrier semaphores. Data moves between devices by JAX's collectives and lax.ppermute only.
A program may use at most 128 MiB of HBM per device.

v0:
```python
import jax
import jax.numpy as jnp
from jax import lax
from jax.sharding import PartitionSpec as P

RG = 8
FIRST_DILATION = 2
SECOND_DILATION = 4
HOPS = 18
sharpness_divisor = 10.0
epsilon = 1e-05


def with_halo(block, sides, width):
    for axis, dim in sides:
        count = lax.axis_size(axis)
        forward = [(i, i + 1) for i in range(count - 1)]
        backward = [(target, source) for source, target in forward]
        low = lax.ppermute(
            lax.slice_in_dim(block, block.shape[dim] - width, None, axis=dim), axis, forward
        )
        high = lax.ppermute(lax.slice_in_dim(block, 0, width, axis=dim), axis, backward)
        block = jnp.concatenate([low, block, high], axis=dim)
    return block


def convolution_layer(images, weights, dilation):
    padded = with_halo(images, (("rows", 2), ("cols", 3)), dilation)
    height = images.shape[2]
    full_width = images.shape[3]
    summed = jnp.zeros((images.shape[0], weights.shape[1], height, full_width), jnp.float32)
    for row_tap in range(3):
        for horizontal_offset in range(3):
            window = padded[
                :,
                :,
                row_tap * dilation : row_tap * dilation + height,
                horizontal_offset * dilation : horizontal_offset * dilation + full_width,
            ]
            summed = summed + jnp.einsum(
                "oc,nchw->nohw",
                weights[3 * row_tap + horizontal_offset],
                window,
                preferred_element_type=jnp.float32,
            )
    return summed


def normalize(feature_maps):
    widened = feature_maps.astype(jnp.float32)
    return (
        widened * lax.rsqrt(jnp.mean(widened * widened, axis=1, keepdims=True) + epsilon)
    ).astype(jnp.bfloat16)


def hop_terms(source_descriptors, key_feats, hop_index, low_edge, high_edge):
    plane_total = source_descriptors.shape[0]
    segment = source_descriptors.shape[2]
    pairing_similarity = jnp.einsum(
        "cri,crm->rim", source_descriptors, key_feats, preferred_element_type=jnp.float32
    ) * (sharpness_divisor / plane_total)
    offsets = (
        hop_index * segment
        + lax.broadcasted_iota(jnp.int32, (segment, segment), 0)
        - lax.broadcasted_iota(jnp.int32, (segment, segment), 1)
    )
    inside = (offsets[None] >= low_edge[:, None, None]) & (offsets[None] < high_edge[:, None, None])
    rounded = jnp.where(inside, jnp.exp(pairing_similarity), 0.0).astype(jnp.bfloat16)
    norm_sum = jnp.sum(rounded, axis=-1, dtype=jnp.float32)
    shift_sum = jnp.sum(rounded * offsets.astype(jnp.float32)[None], axis=-1)
    feature_sum = jnp.einsum("rim,crm->cri", rounded, key_feats, preferred_element_type=jnp.float32)
    return (norm_sum, shift_sum, feature_sum)


def per_device(images, first_weight, second_weight, search_ranges):
    inner_activations = jax.nn.silu(convolution_layer(images, first_weight, FIRST_DILATION)).astype(
        jnp.bfloat16
    )
    feature_maps = (
        images.astype(jnp.float32)
        + convolution_layer(inner_activations, second_weight, SECOND_DILATION)
    ).astype(jnp.bfloat16)
    unit_feats = normalize(feature_maps)
    plane_total = unit_feats.shape[1]
    count_rows = unit_feats.shape[2]
    segment = unit_feats.shape[3]
    peer_count = lax.axis_size("cols")
    column = lax.axis_index("cols")
    band_rows = count_rows // peer_count
    full_width = segment * peer_count
    whole_rows = lax.all_to_all(unit_feats, "cols", split_axis=2, concat_axis=3, tiled=True)
    gathered = lax.all_gather(search_ranges, "cols", axis=2, tiled=True)
    spread_rows = jnp.repeat(gathered, RG, axis=1)
    own_ranges = lax.dynamic_slice_in_dim(spread_rows, column * band_rows, band_rows, 1).reshape(
        2, band_rows * peer_count
    )
    low_edge = segment * own_ranges[0]
    high_edge = segment * (own_ranges[0] + own_ranges[1])
    source_descriptors = whole_rows[0].reshape(plane_total, band_rows * peer_count, segment)
    padded = jnp.pad(whole_rows[1], ((0, 0), (0, 0), ((HOPS - 1) * segment, 0)))

    def accumulate(hop_index, carried):
        norm_sum, shift_sum, feature_sum = carried
        key_feats = lax.dynamic_slice_in_dim(
            padded, (HOPS - 1 - hop_index) * segment, full_width, 2
        )
        key_feats = key_feats.reshape(plane_total, band_rows * peer_count, segment)
        new_terms = hop_terms(source_descriptors, key_feats, hop_index, low_edge, high_edge)
        return (norm_sum + new_terms[0], shift_sum + new_terms[1], feature_sum + new_terms[2])

    zero_rows = jnp.zeros((band_rows * peer_count, segment), jnp.float32)
    zero_feats = jnp.zeros((plane_total, band_rows * peer_count, segment), jnp.float32)
    norm_sum, shift_sum, feature_sum = lax.fori_loop(
        0, HOPS, accumulate, (zero_rows, zero_rows, zero_feats)
    )
    matched_rows = (
        (feature_sum / norm_sum[None])
        .astype(jnp.bfloat16)
        .reshape(plane_total, band_rows, full_width)
    )
    disparity_rows = (shift_sum / norm_sum / segment).reshape(band_rows, full_width)
    matched = lax.all_to_all(matched_rows, "cols", split_axis=2, concat_axis=1, tiled=True)
    disparity = lax.all_to_all(disparity_rows, "cols", split_axis=1, concat_axis=0, tiled=True)
    return (matched, disparity)


def solution(mesh):
    placed = (P(None, None, "rows", "cols"), P(), P(), P(None, "rows", "cols"))
    return jax.shard_map(
        per_device,
        mesh=mesh,
        in_specs=placed,
        out_specs=(P(None, "rows", "cols"), P("rows", "cols")),
        check_vma=False,
    )
```

profile of v0, /device:TPU:4, one launch (start us, length us, event | category | flops | bytes accessed | tf_op | source)
XLA Modules:
  0.0 488.2 jit_solution(17448177616877431964)
XLA Ops:
  37.8 4.8 copy.70
  42.7 4.9 fusion.19
  55.2 5.3 %fusion.16 = f32[2,64,128,64]{2,3,1,0:T(8,128)} fusion(bf16[2,64,68,128]{3,1,2,0:T(8,128)(2,1)S(1)} %constant_dynamic-update-slice_fusion, bf16[2,64,68,2]{3,1,2,0:T(8,128)(2,1)} %copy.73, bf16[9,64,64]{2,1,0:T(8,128)(2,1)S(1)} %copy-done.13), kind=kOutput, calls=%fused_computation.40 | convolution fusion | flops 138412032 | bytes 6473728 | tf_op jit(solution)/shard_map/oc,nchw->nohw/dot_general | solution.py:40
  67.2 12.5 %fusion.11 = bf16[2,64,64,128]{3,1,2,0:T(8,128)(2,1)S(1)} fusion(f32[2,64,128,64]{2,3,1,0:T(8,128)} %fusion.44, f32[2,64,128,64]{2,3,1,0:T(8,128)} %fusion.46, f32[2,64,128,64]{2,3,1,0:T(8,128)} %fusion.13, f32[2,64,128,64]{2,3,1,0:T(8,128)} %fusion.64, f32[2,64,128,64]{2,3,1,0:T(8,128)} %fusion.19, f32[2,64,128,64]{2,3,1,0:T(8,128)} %fusion.16, ...), kind=kOutput, calls=%fused_computation.35 | convolution fusion | flops 152043520 | bytes 40124416 | tf_op jit(solution)/shard_map/oc,nchw->nohw/dot_general | solution.py:40
  82.2 16.4 %collective-permute-start.5 = (bf16[2,64,4,128]{3,1,2,0:T(8,128)(2,1)S(1)}, bf16[2,64,4,128]{3,1,2,0:T(8,128)(2,1)S(1)}, u32[]{:S(2)}, u32[]{:S(2)}) collective-permute-start(bf16[2,64,4,128]{3,1,2,0:T(8,128)(2,1)S(1)} %get-tuple-element.205), channel_id=1, source_target_pairs={{8,0},{16,8},{24,16},{9,1},{17,9},{25,17},{10,2},{18,10},{26,18},{... | collective-permute-start | bytes 393224 | tf_op jit(solution)/shard_map/ppermute | solution.py:22
  132.0 5.9 %pad_maximum_fusion = (bf16[2,64,72,132]{3,1,2,0:T(8,128)(2,1)S(1)}, bf16[2,64,72,132]{3,1,2,0:T(8,128)(2,1)S(1)}) fusion(bf16[2,64,72,4]{3,1,2,0:T(8,128)(2,1)} %copy.79, bf16[2,64,4,128]{3,1,2,0:T(8,128)(2,1)S(1)} %collective-permute-done.5, bf16[2,64,64,128]{3,1,2,0:T(8,128)(2,1)S(1)} %copy-done.1, bf16[2,64,4,128]{3,1,2,0:T(8,128)(2,1)S(1)} %collective-permute-done.4, ...), kind=kLoop, calls=%fused_computation.25 | loop fusion | flops 19464192 | bytes 7372800 | tf_op jit(solution)/shard_map/concatenate | solution.py:23
  153.8 15.0 %fusion.5 = (f32[2,64,128]{2,1,0:T(8,128)S(1)}, bf16[2,64,64,128]{3,1,2,0:T(8,128)(2,1)}) fusion(bf16[2,64,72,132]{3,1,2,0:T(8,128)(2,1)} %copy-done.9, bf16[9,64,64]{2,1,0:T(8,128)(2,1)S(1)} %copy-done.14, f32[2,64,128,64]{2,3,1,0:T(8,128)} %fusion.28, f32[2,64,128,64]{2,3,1,0:T(8,128)} %fusion.30, f32[2,64,128,64]{2,3,1,0:T(8,128)} %fusion.32, ...), kind=kOutput, calls=%fused_computation.26 | convolution fusion | flops 148881408 | bytes 39927808 | tf_op jit(solution)/shard_map/oc,nchw->nohw/dot_general | solution.py:40
  172.7 6.6 %all-to-all-start = ((bf16[2,64,64,128]{3,1,0,2:T(8,128)(2,1)}), bf16[2,64,64,128]{3,1,0,2:T(8,128)(2,1)S(1)}, u32[]{:S(2)}, u32[]{:S(2)}) async-start(bf16[2,64,64,128]{3,1,0,2:T(8,128)(2,1)} %copy.80), calls=%async_computation | async-start | bytes 4194304 | tf_op jit(solution)/shard_map/all_to_all | solution.py:91
  179.4 41.5 %all_gather.3 = s32[2,8,8]{1,0,2:T(2,128)S(1)} all-gather(s32[2,8,1]{1,0,2:T(2,128)S(1)} %bitcast.188), channel_id=1, replica_groups=mesh['rows'=4,'cols'=8] {'cols'}, dimensions={2}, use_global_device_ids=true | all-gather | bytes 576 | tf_op jit(solution)/shard_map/all_gather | solution.py:92
  221.1 7.3 %all-to-all-done = bf16[2,64,64,128]{3,1,0,2:T(8,128)(2,1)S(1)} async-done(((bf16[2,64,64,128]{3,1,0,2:T(8,128)(2,1)}), bf16[2,64,64,128]{3,1,0,2:T(8,128)(2,1)S(1)}, u32[]{:S(2)}, u32[]{:S(2)}) %all-to-all-start) | async-done | bytes 2097184 | tf_op jit(solution)/shard_map/all_to_all | solution.py:91
  232.2 204.3 %while.18 = (s32[]{:T(128)}, f32[64,128]{1,0:T(8,128)S(1)}, f32[64,128]{1,0:T(8,128)S(1)}, f32[64,64,128]{2,0,1:T(8,128)}, s32[64]{0:T(128)S(1)}, /*index=5*/s32...) while((s32[]{:T(128)}, f32[64,128]{1,0:T(8,128)S(1)}, ...), condition=%wide.region_4.5_spmd.clone, body=%wide.region_1.4_spmd.clone.sunk | while | flops 280019072 | bytes 33031948 | solution.py:113
  234.1 5.1 %fusion.117 = (f32[64,128]{1,0:T(8,128)S(1)}, f32[64,128]{1,0:T(8,128)S(1)}, bf16[64,128,128]{1,2,0:T(8,128)(2,1)}) fusion(f32[128,128]{0,1:T(8,128)S(1)} %get-tuple-element.268, bf16[64,64,128]{2,0,1:T(8,128)(2,1)} %get-tuple-element.308, bf16[64,64,128]{2,1,0:T(8,128)(2,1)S(1)} %reshape.96, s32[64]{0:T(128)S(1)} %get-tuple-element.306, ...), kind=kOutput, calls=%fused_computation.2.clone.1 | convolution fusion | flops 144687104 | bytes 4391424 | tf_op jit(solution)/shard_map/while/body/eval_jaxpr/cri,crm->rim/dot_general | solution.py:59
  245.4 5.1 %fusion.117 = (f32[64,128]{1,0:T(8,128)S(1)}, f32[64,128]{1,0:T(8,128)S(1)}, bf16[64,128,128]{1,2,0:T(8,128)(2,1)}) fusion(f32[128,128]{0,1:T(8,128)S(1)} %get-tuple-element.268, bf16[64,64,128]{2,0,1:T(8,128)(2,1)} %get-tuple-element.308, bf16[64,64,128]{2,1,0:T(8,128)(2,1)S(1)} %reshape.96, s32[64]{0:T(128)S(1)} %get-tuple-element.306, ...), kind=kOutput, calls=%fused_computation.2.clone.1 | convolution fusion | flops 144687104 | bytes 4391424 | tf_op jit(solution)/shard_map/while/body/eval_jaxpr/cri,crm->rim/dot_general | solution.py:59
  256.8 5.1 %fusion.117 = (f32[64,128]{1,0:T(8,128)S(1)}, f32[64,128]{1,0:T(8,128)S(1)}, bf16[64,128,128]{1,2,0:T(8,128)(2,1)}) fusion(f32[128,128]{0,1:T(8,128)S(1)} %get-tuple-element.268, bf16[64,64,128]{2,0,1:T(8,128)(2,1)} %get-tuple-element.308, bf16[64,64,128]{2,1,0:T(8,128)(2,1)S(1)} %reshape.96, s32[64]{0:T(128)S(1)} %get-tuple-element.306, ...), kind=kOutput, calls=%fused_computation.2.clone.1 | convolution fusion | flops 144687104 | bytes 4391424 | tf_op jit(solution)/shard_map/while/body/eval_jaxpr/cri,crm->rim/dot_general | solution.py:59
  268.1 5.1 %fusion.117 = (f32[64,128]{1,0:T(8,128)S(1)}, f32[64,128]{1,0:T(8,128)S(1)}, bf16[64,128,128]{1,2,0:T(8,128)(2,1)}) fusion(f32[128,128]{0,1:T(8,128)S(1)} %get-tuple-element.268, bf16[64,64,128]{2,0,1:T(8,128)(2,1)} %get-tuple-element.308, bf16[64,64,128]{2,1,0:T(8,128)(2,1)S(1)} %reshape.96, s32[64]{0:T(128)S(1)} %get-tuple-element.306, ...), kind=kOutput, calls=%fused_computation.2.clone.1 | convolution fusion | flops 144687104 | bytes 4391424 | tf_op jit(solution)/shard_map/while/body/eval_jaxpr/cri,crm->rim/dot_general | solution.py:59
  279.5 5.1 %fusion.117 = (f32[64,128]{1,0:T(8,128)S(1)}, f32[64,128]{1,0:T(8,128)S(1)}, bf16[64,128,128]{1,2,0:T(8,128)(2,1)}) fusion(f32[128,128]{0,1:T(8,128)S(1)} %get-tuple-element.268, bf16[64,64,128]{2,0,1:T(8,128)(2,1)} %get-tuple-element.308, bf16[64,64,128]{2,1,0:T(8,128)(2,1)S(1)} %reshape.96, s32[64]{0:T(128)S(1)} %get-tuple-element.306, ...), kind=kOutput, calls=%fused_computation.2.clone.1 | convolution fusion | flops 144687104 | bytes 4391424 | tf_op jit(solution)/shard_map/while/body/eval_jaxpr/cri,crm->rim/dot_general | solution.py:59
  290.8 5.1 %fusion.117 = (f32[64,128]{1,0:T(8,128)S(1)}, f32[64,128]{1,0:T(8,128)S(1)}, bf16[64,128,128]{1,2,0:T(8,128)(2,1)}) fusion(f32[128,128]{0,1:T(8,128)S(1)} %get-tuple-element.268, bf16[64,64,128]{2,0,1:T(8,128)(2,1)} %get-tuple-element.308, bf16[64,64,128]{2,1,0:T(8,128)(2,1)S(1)} %reshape.96, s32[64]{0:T(128)S(1)} %get-tuple-element.306, ...), kind=kOutput, calls=%fused_computation.2.clone.1 | convolution fusion | flops 144687104 | bytes 4391424 | tf_op jit(solution)/shard_map/while/body/eval_jaxpr/cri,crm->rim/dot_general | solution.py:59
  302.2 5.1 %fusion.117 = (f32[64,128]{1,0:T(8,128)S(1)}, f32[64,128]{1,0:T(8,128)S(1)}, bf16[64,128,128]{1,2,0:T(8,128)(2,1)}) fusion(f32[128,128]{0,1:T(8,128)S(1)} %get-tuple-element.268, bf16[64,64,128]{2,0,1:T(8,128)(2,1)} %get-tuple-element.308, bf16[64,64,128]{2,1,0:T(8,128)(2,1)S(1)} %reshape.96, s32[64]{0:T(128)S(1)} %get-tuple-element.306, ...), kind=kOutput, calls=%fused_computation.2.clone.1 | convolution fusion | flops 144687104 | bytes 4391424 | tf_op jit(solution)/shard_map/while/body/eval_jaxpr/cri,crm->rim/dot_general | solution.py:59
  313.5 5.1 %fusion.117 = (f32[64,128]{1,0:T(8,128)S(1)}, f32[64,128]{1,0:T(8,128)S(1)}, bf16[64,128,128]{1,2,0:T(8,128)(2,1)}) fusion(f32[128,128]{0,1:T(8,128)S(1)} %get-tuple-element.268, bf16[64,64,128]{2,0,1:T(8,128)(2,1)} %get-tuple-element.308, bf16[64,64,128]{2,1,0:T(8,128)(2,1)S(1)} %reshape.96, s32[64]{0:T(128)S(1)} %get-tuple-element.306, ...), kind=kOutput, calls=%fused_computation.2.clone.1 | convolution fusion | flops 144687104 | bytes 4391424 | tf_op jit(solution)/shard_map/while/body/eval_jaxpr/cri,crm->rim/dot_general | solution.py:59
  324.9 5.1 %fusion.117 = (f32[64,128]{1,0:T(8,128)S(1)}, f32[64,128]{1,0:T(8,128)S(1)}, bf16[64,128,128]{1,2,0:T(8,128)(2,1)}) fusion(f32[128,128]{0,1:T(8,128)S(1)} %get-tuple-element.268, bf16[64,64,128]{2,0,1:T(8,128)(2,1)} %get-tuple-element.308, bf16[64,64,128]{2,1,0:T(8,128)(2,1)S(1)} %reshape.96, s32[64]{0:T(128)S(1)} %get-tuple-element.306, ...), kind=kOutput, calls=%fused_computation.2.clone.1 | convolution fusion | flops 144687104 | bytes 4391424 | tf_op jit(solution)/shard_map/while/body/eval_jaxpr/cri,crm->rim/dot_general | solution.py:59
  336.2 5.1 %fusion.117 = (f32[64,128]{1,0:T(8,128)S(1)}, f32[64,128]{1,0:T(8,128)S(1)}, bf16[64,128,128]{1,2,0:T(8,128)(2,1)}) fusion(f32[128,128]{0,1:T(8,128)S(1)} %get-tuple-element.268, bf16[64,64,128]{2,0,1:T(8,128)(2,1)} %get-tuple-element.308, bf16[64,64,128]{2,1,0:T(8,128)(2,1)S(1)} %reshape.96, s32[64]{0:T(128)S(1)} %get-tuple-element.306, ...), kind=kOutput, calls=%fused_computation.2.clone.1 | convolution fusion | flops 144687104 | bytes 4391424 | tf_op jit(solution)/shard_map/while/body/eval_jaxpr/cri,crm->rim/dot_general | solution.py:59
  347.6 5.1 %fusion.117 = (f32[64,128]{1,0:T(8,128)S(1)}, f32[64,128]{1,0:T(8,128)S(1)}, bf16[64,128,128]{1,2,0:T(8,128)(2,1)}) fusion(f32[128,128]{0,1:T(8,128)S(1)} %get-tuple-element.268, bf16[64,64,128]{2,0,1:T(8,128)(2,1)} %get-tuple-element.308, bf16[64,64,128]{2,1,0:T(8,128)(2,1)S(1)} %reshape.96, s32[64]{0:T(128)S(1)} %get-tuple-element.306, ...), kind=kOutput, calls=%fused_computation.2.clone.1 | convolution fusion | flops 144687104 | bytes 4391424 | tf_op jit(solution)/shard_map/while/body/eval_jaxpr/cri,crm->rim/dot_general | solution.py:59
  358.9 5.1 %fusion.117 = (f32[64,128]{1,0:T(8,128)S(1)}, f32[64,128]{1,0:T(8,128)S(1)}, bf16[64,128,128]{1,2,0:T(8,128)(2,1)}) fusion(f32[128,128]{0,1:T(8,128)S(1)} %get-tuple-element.268, bf16[64,64,128]{2,0,1:T(8,128)(2,1)} %get-tuple-element.308, bf16[64,64,128]{2,1,0:T(8,128)(2,1)S(1)} %reshape.96, s32[64]{0:T(128)S(1)} %get-tuple-element.306, ...), kind=kOutput, calls=%fused_computation.2.clone.1 | convolution fusion | flops 144687104 | bytes 4391424 | tf_op jit(solution)/shard_map/while/body/eval_jaxpr/cri,crm->rim/dot_general | solution.py:59
  370.3 5.1 %fusion.117 = (f32[64,128]{1,0:T(8,128)S(1)}, f32[64,128]{1,0:T(8,128)S(1)}, bf16[64,128,128]{1,2,0:T(8,128)(2,1)}) fusion(f32[128,128]{0,1:T(8,128)S(1)} %get-tuple-element.268, bf16[64,64,128]{2,0,1:T(8,128)(2,1)} %get-tuple-element.308, bf16[64,64,128]{2,1,0:T(8,128)(2,1)S(1)} %reshape.96, s32[64]{0:T(128)S(1)} %get-tuple-element.306, ...), kind=kOutput, calls=%fused_computation.2.clone.1 | convolution fusion | flops 144687104 | bytes 4391424 | tf_op jit(solution)/shard_map/while/body/eval_jaxpr/cri,crm->rim/dot_general | solution.py:59
  381.6 5.1 %fusion.117 = (f32[64,128]{1,0:T(8,128)S(1)}, f32[64,128]{1,0:T(8,128)S(1)}, bf16[64,128,128]{1,2,0:T(8,128)(2,1)}) fusion(f32[128,128]{0,1:T(8,128)S(1)} %get-tuple-element.268, bf16[64,64,128]{2,0,1:T(8,128)(2,1)} %get-tuple-element.308, bf16[64,64,128]{2,1,0:T(8,128)(2,1)S(1)} %reshape.96, s32[64]{0:T(128)S(1)} %get-tuple-element.306, ...), kind=kOutput, calls=%fused_computation.2.clone.1 | convolution fusion | flops 144687104 | bytes 4391424 | tf_op jit(solution)/shard_map/while/body/eval_jaxpr/cri,crm->rim/dot_general | solution.py:59
  393.0 5.1 %fusion.117 = (f32[64,128]{1,0:T(8,128)S(1)}, f32[64,128]{1,0:T(8,128)S(1)}, bf16[64,128,128]{1,2,0:T(8,128)(2,1)}) fusion(f32[128,128]{0,1:T(8,128)S(1)} %get-tuple-element.268, bf16[64,64,128]{2,0,1:T(8,128)(2,1)} %get-tuple-element.308, bf16[64,64,128]{2,1,0:T(8,128)(2,1)S(1)} %reshape.96, s32[64]{0:T(128)S(1)} %get-tuple-element.306, ...), kind=kOutput, calls=%fused_computation.2.clone.1 | convolution fusion | flops 144687104 | bytes 4391424 | tf_op jit(solution)/shard_map/while/body/eval_jaxpr/cri,crm->rim/dot_general | solution.py:59
  404.3 5.1 %fusion.117 = (f32[64,128]{1,0:T(8,128)S(1)}, f32[64,128]{1,0:T(8,128)S(1)}, bf16[64,128,128]{1,2,0:T(8,128)(2,1)}) fusion(f32[128,128]{0,1:T(8,128)S(1)} %get-tuple-element.268, bf16[64,64,128]{2,0,1:T(8,128)(2,1)} %get-tuple-element.308, bf16[64,64,128]{2,1,0:T(8,128)(2,1)S(1)} %reshape.96, s32[64]{0:T(128)S(1)} %get-tuple-element.306, ...), kind=kOutput, calls=%fused_computation.2.clone.1 | convolution fusion | flops 144687104 | bytes 4391424 | tf_op jit(solution)/shard_map/while/body/eval_jaxpr/cri,crm->rim/dot_general | solution.py:59
  415.7 5.1 %fusion.117 = (f32[64,128]{1,0:T(8,128)S(1)}, f32[64,128]{1,0:T(8,128)S(1)}, bf16[64,128,128]{1,2,0:T(8,128)(2,1)}) fusion(f32[128,128]{0,1:T(8,128)S(1)} %get-tuple-element.268, bf16[64,64,128]{2,0,1:T(8,128)(2,1)} %get-tuple-element.308, bf16[64,64,128]{2,1,0:T(8,128)(2,1)S(1)} %reshape.96, s32[64]{0:T(128)S(1)} %get-tuple-element.306, ...), kind=kOutput, calls=%fused_computation.2.clone.1 | convolution fusion | flops 144687104 | bytes 4391424 | tf_op jit(solution)/shard_map/while/body/eval_jaxpr/cri,crm->rim/dot_general | solution.py:59
  427.0 5.1 %fusion.117 = (f32[64,128]{1,0:T(8,128)S(1)}, f32[64,128]{1,0:T(8,128)S(1)}, bf16[64,128,128]{1,2,0:T(8,128)(2,1)}) fusion(f32[128,128]{0,1:T(8,128)S(1)} %get-tuple-element.268, bf16[64,64,128]{2,0,1:T(8,128)(2,1)} %get-tuple-element.308, bf16[64,64,128]{2,1,0:T(8,128)(2,1)S(1)} %reshape.96, s32[64]{0:T(128)S(1)} %get-tuple-element.306, ...), kind=kOutput, calls=%fused_computation.2.clone.1 | convolution fusion | flops 144687104 | bytes 4391424 | tf_op jit(solution)/shard_map/while/body/eval_jaxpr/cri,crm->rim/dot_general | solution.py:59
  437.2 5.9 %all-to-all-start.2 = ((f32[8,8,128]{2,0,1:T(8,128)}), f32[8,8,128]{2,0,1:T(8,128)S(1)}, u32[]{:S(2)}, u32[]{:S(2)}) async-start(f32[8,8,128]{2,0,1:T(8,128)} %copy.86), calls=%async_computation.2 | async-start | bytes 65536 | tf_op jit(solution)/shard_map/all_to_all | solution.py:123
  451.1 5.1 %all-to-all-start.1 = ((bf16[8,2,32768]{2,1,0:T(2,128)(2,1)}), bf16[8,2,32768]{2,1,0:T(2,128)(2,1)S(1)}, u32[]{:S(2)}, u32[]{:S(2)}) async-start(bf16[8,2,32768]{2,1,0:T(2,128)(2,1)} %reshape.93), calls=%async_computation.1 | async-start | bytes 2097152 | tf_op jit(solution)/shard_map/all_to_all | solution.py:122
  456.2 26.6 %all-to-all-done.1 = bf16[8,2,32768]{2,1,0:T(2,128)(2,1)S(1)} async-done(((bf16[8,2,32768]{2,1,0:T(2,128)(2,1)}), bf16[8,2,32768]{2,1,0:T(2,128)(2,1)S(1)}, u32[]{:S(2)}, u32[]{:S(2)}) %all-to-all-start.1) | async-done | bytes 1048608 | tf_op jit(solution)/shard_map/all_to_all | solution.py:122
  (279 shorter events, 235.3 us)
Async XLA Ops:
  0.6 9.9 %copy-start.7 = (bf16[2,64,64,128]{3,2,1,0:T(8,128)(2,1)S(1)}, bf16[2,64,64,128]{3,2,1,0:T(8,128)(2,1)}, u32[]{:S(2)}) copy-start(bf16[2,64,64,128]{3,2,1,0:T(8,128)(2,1)} %param.6) | copy-start | bytes 6291460
  0.6 9.9 %copy-start.13 = (bf16[9,64,64]{2,1,0:T(8,128)(2,1)S(1)}, bf16[9,64,64]{2,1,0:T(8,128)(2,1)}, u32[]{:S(2)}) copy-start(bf16[9,64,64]{2,1,0:T(8,128)(2,1)} %param.7) | copy-start | bytes 221188
  3.7 12.0 %copy-start.10 = (bf16[2,64,64,128]{3,1,2,0:T(8,128)(2,1)}, bf16[2,64,64,128]{3,1,2,0:T(8,128)(2,1)S(1)}, u32[]{:S(2)}) copy-start(bf16[2,64,64,128]{3,1,2,0:T(8,128)(2,1)S(1)} %copy.65) | copy-start | bytes 6291460
  3.8 10.4 %collective-permute-start = (bf16[2,64,2,128]{3,1,2,0:T(8,128)(2,1)S(1)}, bf16[2,64,2,128]{3,1,2,0:T(8,128)(2,1)S(1)}, u32[]{:S(2)}, u32[]{:S(2)}) collective-permute-start(bf16[2,64,2,128]{3,1,2,0:T(8,128)(2,1)S(1)} %get-tuple-element.206), channel_id=1, source_target_pairs={{0,8},{8,16},{16,24},{1,9},{9,17},{17,25},{2,10},{10,18},{18,26},{... | collective-permute-start | bytes 196616 | tf_op jit(solution)/shard_map/ppermute | solution.py:19
  7.2 8.5 %collective-permute-start.1 = (bf16[2,64,2,128]{3,1,2,0:T(8,128)(2,1)S(1)}, bf16[2,64,2,128]{3,1,2,0:T(8,128)(2,1)S(1)}, u32[]{:S(2)}, u32[]{:S(2)}) collective-permute-start(bf16[2,64,2,128]{3,1,2,0:T(8,128)(2,1)S(1)} %get-tuple-element.207), channel_id=1, source_target_pairs={{8,0},{16,8},{24,16},{9,1},{17,9},{25,17},{10,2},{18,10},{26,18},{... | collective-permute-start | bytes 196616 | tf_op jit(solution)/shard_map/ppermute | solution.py:22
  22.7 28.0 %collective-permute-start.3 = (bf16[2,64,68,2]{2,1,3,0:T(8,128)(2,1)S(1)}, bf16[2,64,68,2]{2,1,3,0:T(8,128)(2,1)S(1)}, u32[]{:S(2)}, u32[]{:S(2)}) collective-permute-start(bf16[2,64,68,2]{2,1,3,0:T(8,128)(2,1)S(1)} %copy.72), channel_id=1, source_target_pairs={{1,0},{2,1},{3,2},{4,3},{5,4},{6,5},{7,6},{9,8},{10,9},{11,10},{12... | collective-permute-start | bytes 104456 | tf_op jit(solution)/shard_map/ppermute | solution.py:22
  27.7 7.5 %copy-start.11 = (bf16[2,64,64,128]{3,1,2,0:T(8,128)(2,1)S(1)}, bf16[2,64,64,128]{3,1,2,0:T(8,128)(2,1)}, u32[]{:S(2)}) copy-start(bf16[2,64,64,128]{3,1,2,0:T(8,128)(2,1)} %copy-done.10) | copy-start | bytes 6291460
  27.7 10.1 %collective-permute-start.2 = (bf16[2,64,68,2]{2,1,3,0:T(8,128)(2,1)S(1)}, bf16[2,64,68,2]{2,1,3,0:T(8,128)(2,1)S(1)}, u32[]{:S(2)}, u32[]{:S(2)}) collective-permute-start(bf16[2,64,68,2]{2,1,3,0:T(8,128)(2,1)S(1)} %copy.69), channel_id=1, source_target_pairs={{0,1},{1,2},{2,3},{3,4},{4,5},{5,6},{6,7},{8,9},{9,10},{10,11},{11... | collective-permute-start | bytes 104456 | tf_op jit(solution)/shard_map/ppermute | solution.py:19
  55.2 5.3 %copy-start.4 = (bf16[2,64,68,2]{3,1,2,0:T(8,128)(2,1)S(1)}, bf16[2,64,68,2]{3,1,2,0:T(8,128)(2,1)}, u32[]{:S(2)}) copy-start(bf16[2,64,68,2]{3,1,2,0:T(8,128)(2,1)} %copy.73) | copy-start | bytes 104452
  67.1 31.5 %copy-start.14 = (bf16[9,64,64]{2,1,0:T(8,128)(2,1)S(1)}, bf16[9,64,64]{2,1,0:T(8,128)(2,1)}, u32[]{:S(2)}) copy-start(bf16[9,64,64]{2,1,0:T(8,128)(2,1)} %param.8) | copy-start | bytes 221188
  79.7 22.0 %copy-start = (bf16[2,64,64,128]{3,1,2,0:T(8,128)(2,1)}, bf16[2,64,64,128]{3,1,2,0:T(8,128)(2,1)S(1)}, u32[]{:S(2)}) copy-start(bf16[2,64,64,128]{3,1,2,0:T(8,128)(2,1)S(1)} %fusion.11) | copy-start | bytes 6291460
  79.7 21.6 %collective-permute-start.4 = (bf16[2,64,4,128]{3,1,2,0:T(8,128)(2,1)S(1)}, bf16[2,64,4,128]{3,1,2,0:T(8,128)(2,1)S(1)}, u32[]{:S(2)}, u32[]{:S(2)}) collective-permute-start(bf16[2,64,4,128]{3,1,2,0:T(8,128)(2,1)S(1)} %get-tuple-element.204), channel_id=1, source_target_pairs={{0,8},{8,16},{16,24},{1,9},{9,17},{17,25},{2,10},{10,18},{18,26},{... | collective-permute-start | bytes 393224 | tf_op jit(solution)/shard_map/ppermute | solution.py:19
  82.2 19.1 %collective-permute-start.5 = (bf16[2,64,4,128]{3,1,2,0:T(8,128)(2,1)S(1)}, bf16[2,64,4,128]{3,1,2,0:T(8,128)(2,1)S(1)}, u32[]{:S(2)}, u32[]{:S(2)}) collective-permute-start(bf16[2,64,4,128]{3,1,2,0:T(8,128)(2,1)S(1)} %get-tuple-element.205), channel_id=1, source_target_pairs={{8,0},{16,8},{24,16},{9,1},{17,9},{25,17},{10,2},{18,10},{26,18},{... | collective-permute-start | bytes 393224 | tf_op jit(solution)/shard_map/ppermute | solution.py:22
  105.0 12.1 %copy-start.1 = (bf16[2,64,64,128]{3,1,2,0:T(8,128)(2,1)S(1)}, bf16[2,64,64,128]{3,1,2,0:T(8,128)(2,1)}, u32[]{:S(2)}) copy-start(bf16[2,64,64,128]{3,1,2,0:T(8,128)(2,1)} %copy-done) | copy-start | bytes 6291460
  109.2 13.3 %collective-permute-start.6 = (bf16[2,64,72,4]{2,1,3,0:T(8,128)(2,1)S(1)}, bf16[2,64,72,4]{2,1,3,0:T(8,128)(2,1)S(1)}, u32[]{:S(2)}, u32[]{:S(2)}) collective-permute-start(bf16[2,64,72,4]{2,1,3,0:T(8,128)(2,1)S(1)} %copy.76), channel_id=1, source_target_pairs={{0,1},{1,2},{2,3},{3,4},{4,5},{5,6},{6,7},{8,9},{9,10},{10,11},{11... | collective-permute-start | bytes 221192 | tf_op jit(solution)/shard_map/ppermute | solution.py:19
  115.8 11.4 %collective-permute-start.7 = (bf16[2,64,72,4]{2,1,3,0:T(8,128)(2,1)S(1)}, bf16[2,64,72,4]{2,1,3,0:T(8,128)(2,1)S(1)}, u32[]{:S(2)}, u32[]{:S(2)}) collective-permute-start(bf16[2,64,72,4]{2,1,3,0:T(8,128)(2,1)S(1)} %copy.78), channel_id=1, source_target_pairs={{1,0},{2,1},{3,2},{4,3},{5,4},{6,5},{7,6},{9,8},{10,9},{11,10},{12... | collective-permute-start | bytes 221192 | tf_op jit(solution)/shard_map/ppermute | solution.py:22
  137.9 8.8 %copy-start.9 = (bf16[2,64,72,132]{3,1,2,0:T(8,128)(2,1)}, bf16[2,64,72,132]{3,1,2,0:T(8,128)(2,1)S(1)}, u32[]{:S(2)}) copy-start(bf16[2,64,72,132]{3,1,2,0:T(8,128)(2,1)S(1)} %get-tuple-element.196) | copy-start | bytes 7299076
  171.1 8.2 %copy-start.15 = (s32[2,8,1]{1,2,0:T(1,128)S(1)}, s32[2,8,1]{1,2,0:T(1,128)}, u32[]{:S(2)}) copy-start(s32[2,8,1]{1,2,0:T(1,128)} %param.9) | copy-start | bytes 196
  172.7 55.7 %all-to-all-start = ((bf16[2,64,64,128]{3,1,0,2:T(8,128)(2,1)}), bf16[2,64,64,128]{3,1,0,2:T(8,128)(2,1)S(1)}, u32[]{:S(2)}, u32[]{:S(2)}) async-start(bf16[2,64,64,128]{3,1,0,2:T(8,128)(2,1)} %copy.80), calls=%async_computation | async-start | bytes 4194304 | tf_op jit(solution)/shard_map/all_to_all | solution.py:91
  245.4 5.2 %copy-start.2 = (f32[64,64,128]{2,0,1:T(8,128)S(1)}, f32[64,64,128]{2,0,1:T(8,128)}, u32[]{:S(2)}) copy-start(f32[64,64,128]{2,0,1:T(8,128)} %get-tuple-element.291) | copy-start | bytes 6291460 | tf_op jit(solution)/shard_map/while
  256.7 5.2 %copy-start.2 = (f32[64,64,128]{2,0,1:T(8,128)S(1)}, f32[64,64,128]{2,0,1:T(8,128)}, u32[]{:S(2)}) copy-start(f32[64,64,128]{2,0,1:T(8,128)} %get-tuple-element.291) | copy-start | bytes 6291460 | tf_op jit(solution)/shard_map/while
  268.1 5.2 %copy-start.2 = (f32[64,64,128]{2,0,1:T(8,128)S(1)}, f32[64,64,128]{2,0,1:T(8,128)}, u32[]{:S(2)}) copy-start(f32[64,64,128]{2,0,1:T(8,128)} %get-tuple-element.291) | copy-start | bytes 6291460 | tf_op jit(solution)/shard_map/while
  279.4 5.2 %copy-start.2 = (f32[64,64,128]{2,0,1:T(8,128)S(1)}, f32[64,64,128]{2,0,1:T(8,128)}, u32[]{:S(2)}) copy-start(f32[64,64,128]{2,0,1:T(8,128)} %get-tuple-element.291) | copy-start | bytes 6291460 | tf_op jit(solution)/shard_map/while
  290.8 5.2 %copy-start.2 = (f32[64,64,128]{2,0,1:T(8,128)S(1)}, f32[64,64,128]{2,0,1:T(8,128)}, u32[]{:S(2)}) copy-start(f32[64,64,128]{2,0,1:T(8,128)} %get-tuple-element.291) | copy-start | bytes 6291460 | tf_op jit(solution)/shard_map/while
  336.2 5.2 %copy-start.2 = (f32[64,64,128]{2,0,1:T(8,128)S(1)}, f32[64,64,128]{2,0,1:T(8,128)}, u32[]{:S(2)}) copy-start(f32[64,64,128]{2,0,1:T(8,128)} %get-tuple-element.291) | copy-start | bytes 6291460 | tf_op jit(solution)/shard_map/while
  347.6 5.2 %copy-start.2 = (f32[64,64,128]{2,0,1:T(8,128)S(1)}, f32[64,64,128]{2,0,1:T(8,128)}, u32[]{:S(2)}) copy-start(f32[64,64,128]{2,0,1:T(8,128)} %get-tuple-element.291) | copy-start | bytes 6291460 | tf_op jit(solution)/shard_map/while
  358.9 5.2 %copy-start.2 = (f32[64,64,128]{2,0,1:T(8,128)S(1)}, f32[64,64,128]{2,0,1:T(8,128)}, u32[]{:S(2)}) copy-start(f32[64,64,128]{2,0,1:T(8,128)} %get-tuple-element.291) | copy-start | bytes 6291460 | tf_op jit(solution)/shard_map/while
  370.3 5.2 %copy-start.2 = (f32[64,64,128]{2,0,1:T(8,128)S(1)}, f32[64,64,128]{2,0,1:T(8,128)}, u32[]{:S(2)}) copy-start(f32[64,64,128]{2,0,1:T(8,128)} %get-tuple-element.291) | copy-start | bytes 6291460 | tf_op jit(solution)/shard_map/while
  381.6 5.2 %copy-start.2 = (f32[64,64,128]{2,0,1:T(8,128)S(1)}, f32[64,64,128]{2,0,1:T(8,128)}, u32[]{:S(2)}) copy-start(f32[64,64,128]{2,0,1:T(8,128)} %get-tuple-element.291) | copy-start | bytes 6291460 | tf_op jit(solution)/shard_map/while
  393.0 5.2 %copy-start.2 = (f32[64,64,128]{2,0,1:T(8,128)S(1)}, f32[64,64,128]{2,0,1:T(8,128)}, u32[]{:S(2)}) copy-start(f32[64,64,128]{2,0,1:T(8,128)} %get-tuple-element.291) | copy-start | bytes 6291460 | tf_op jit(solution)/shard_map/while
  437.2 13.9 %all-to-all-start.2 = ((f32[8,8,128]{2,0,1:T(8,128)}), f32[8,8,128]{2,0,1:T(8,128)S(1)}, u32[]{:S(2)}, u32[]{:S(2)}) async-start(f32[8,8,128]{2,0,1:T(8,128)} %copy.86), calls=%async_computation.2 | async-start | bytes 65536 | tf_op jit(solution)/shard_map/all_to_all | solution.py:123
  451.1 31.7 %all-to-all-start.1 = ((bf16[8,2,32768]{2,1,0:T(2,128)(2,1)}), bf16[8,2,32768]{2,1,0:T(2,128)(2,1)S(1)}, u32[]{:S(2)}, u32[]{:S(2)}) async-start(bf16[8,2,32768]{2,1,0:T(2,128)(2,1)} %reshape.93), calls=%async_computation.1 | async-start | bytes 2097152 | tf_op jit(solution)/shard_map/all_to_all | solution.py:122
  (29 other events, 75.7 us)
where the time goes:
time: 497 us; the launch traced here: 488 us
  matrix products  227 us (46%)
  local copies, waits for them, and re-layouts  120 us (24%)
  starting transfers between devices  51.6 us (10%)
  blocking collectives  41.5 us (8%)
  waiting for transfers between devices  33.9 us (7%)
  other arithmetic  11 us (2%)
    dot_general x18, matrix products, hop_terms(): jnp.einsum('cri,crm->rim', source_descriptors, key_feats, preferred_eleme...  92.6 us
    dot_general x18, matrix products, convolution_layer(): jnp.einsum('oc,nchw->nohw', weights[3 * row_tap + horizontal_offset], win...  80.5 us
    dot_general x18, matrix products, hop_terms(): jnp.einsum('rim,crm->cri', rounded, key_feats, preferred_element_type=jnp...  54.3 us
    all_gather x1, blocking collectives, per_device(): gathered = lax.all_gather(search_ranges, 'cols', axis=2, tiled=True)  41.5 us
    all_to_all x1, waiting for transfers between devices, per_device(): lax.all_to_all(matched_rows, 'cols', split_axis=2, concat_axis=1, tiled=T...  26.6 us
    while x72, local copies, waits for them, and re-layouts  23.5 us
    dynamic_slice x18, local copies, waits for them, and re-layouts, accumulate(): lax.dynamic_slice_in_dim(padded, (HOPS - 1 - hop_index) * segment, full_w...  23.3 us
    ppermute x4, starting transfers between devices, with_halo(): lax.ppermute(lax.slice_in_dim(block, 0, width, axis=dim), axis, backward)  22.3 us
  transfers between devices with their start and end apart: 11, of which 2 were waited for; matrix products, arithmetic and copies ran while one was open for 11% of the time, Pallas kernels for 0%

commit v1 on v0

--- a/solution.py
+++ b/solution.py
@@ -89,7 +89,12 @@
     band_rows = count_rows // peer_count
     full_width = segment * peer_count
     whole_rows = lax.all_to_all(unit_feats, "cols", split_axis=2, concat_axis=3, tiled=True)
-    gathered = lax.all_gather(search_ranges, "cols", axis=2, tiled=True)
+    ring = [search_ranges]
+    for hop in range(7):
+        ring.append(lax.ppermute(ring[-1], "cols", [(dev, (dev + 1) % 8) for dev in range(8)]))
+    gathered = jnp.roll(
+        jnp.concatenate(ring[::-1], axis=2), (lax.axis_index("cols") + 1) * ring[0].shape[2], axis=2
+    )
     spread_rows = jnp.repeat(gathered, RG, axis=1)
     own_ranges = lax.dynamic_slice_in_dim(spread_rows, column * band_rows, band_rows, 1).reshape(
         2, band_rows * peer_count

time: 497 us -> 513 us (1.032)
  waiting for transfers between devices: 33.9 us -> 91.7 us
  blocking collectives: 41.5 us -> 0 us
    ppermute x0 -> x7, waiting for transfers between devices: none -> 65.1 us  [per_device(): lax.ppermute(ring[-1], 'cols', [(dev, (dev + 1) % 8) for dev in range(8)])]
    all_gather x1 -> x0, blocking collectives: 41.5 us -> none  [per_device(): gathered = lax.all_gather(search_ranges, 'cols', axis=2, tiled=True)]
    all_to_all x1, waiting for transfers between devices: 7.28 us -> 0.01 us  [per_device(): lax.all_to_all(unit_feats, 'cols', split_axis=2, concat_axis=3, tiled=True)]
  transfers between devices with their start and end apart: 11 -> 18, of which waited for: 2 -> 8; matrix products, arithmetic and copies ran while one was open for 11% -> 11% of each run, Pallas kernels for 0% -> 0%
where the time goes in v1:
time: 513 us; the launch traced here: 504 us
  matrix products  227 us (44%)
  local copies, waits for them, and re-layouts  120 us (23%)
  waiting for transfers between devices  91.7 us (18%)
  starting transfers between devices  51.5 us (10%)
  other arithmetic  11 us (2%)
    dot_general x18, matrix products, hop_terms(): jnp.einsum('cri,crm->rim', source_descriptors, key_feats, preferred_eleme...  92.3 us
    dot_general x18, matrix products, convolution_layer(): jnp.einsum('oc,nchw->nohw', weights[3 * row_tap + horizontal_offset], win...  80.7 us
    ppermute x7, waiting for transfers between devices, per_device(): lax.ppermute(ring[-1], 'cols', [(dev, (dev + 1) % 8) for dev in range(8)])  65.1 us
    dot_general x18, matrix products, hop_terms(): jnp.einsum('rim,crm->cri', rounded, key_feats, preferred_element_type=jnp...  54.2 us
    all_to_all x1, waiting for transfers between devices, per_device(): lax.all_to_all(matched_rows, 'cols', split_axis=2, concat_axis=1, tiled=T...  26.6 us
    while x72, local copies, waits for them, and re-layouts  23.5 us
    dynamic_slice x18, local copies, waits for them, and re-layouts, accumulate(): lax.dynamic_slice_in_dim(padded, (HOPS - 1 - hop_index) * segment, full_w...  23.3 us
    ppermute x4, starting transfers between devices, with_halo(): lax.ppermute(lax.slice_in_dim(block, 0, width, axis=dim), axis, backward)  22.8 us
  transfers between devices with their start and end apart: 18, of which 8 were waited for; matrix products, arithmetic and copies ran while one was open for 11% of the time, Pallas kernels for 0%

profile of v1, /device:TPU:4, one launch (start us, length us, event | category | flops | bytes accessed | tf_op | source)
XLA Modules:
  0.0 504.3 jit_solution(3718636443606451689)
XLA Ops:
  37.9 4.8 copy.68
  42.7 4.9 fusion.19
  55.2 5.3 %fusion.16 = f32[2,64,128,64]{2,3,1,0:T(8,128)} fusion(bf16[2,64,68,128]{3,1,2,0:T(8,128)(2,1)S(1)} %constant_dynamic-update-slice_fusion, bf16[2,64,68,2]{3,1,2,0:T(8,128)(2,1)} %copy.71, bf16[9,64,64]{2,1,0:T(8,128)(2,1)S(1)} %copy-done.13), kind=kOutput, calls=%fused_computation.40 | convolution fusion | flops 138412032 | bytes 6473728 | tf_op jit(solution)/shard_map/oc,nchw->nohw/dot_general | solution.py:40
  67.2 12.5 %fusion.11 = bf16[2,64,64,128]{3,1,2,0:T(8,128)(2,1)S(1)} fusion(f32[2,64,128,64]{2,3,1,0:T(8,128)} %fusion.44, f32[2,64,128,64]{2,3,1,0:T(8,128)} %fusion.46, f32[2,64,128,64]{2,3,1,0:T(8,128)} %fusion.13, f32[2,64,128,64]{2,3,1,0:T(8,128)} %fusion.64, f32[2,64,128,64]{2,3,1,0:T(8,128)} %fusion.19, f32[2,64,128,64]{2,3,1,0:T(8,128)} %fusion.16, ...), kind=kOutput, calls=%fused_computation.35 | convolution fusion | flops 152043520 | bytes 40124416 | tf_op jit(solution)/shard_map/oc,nchw->nohw/dot_general | solution.py:40
  82.3 16.8 %collective-permute-start.12 = (bf16[2,64,4,128]{3,1,2,0:T(8,128)(2,1)S(1)}, bf16[2,64,4,128]{3,1,2,0:T(8,128)(2,1)S(1)}, u32[]{:S(2)}, u32[]{:S(2)}) collective-permute-start(bf16[2,64,4,128]{3,1,2,0:T(8,128)(2,1)S(1)} %get-tuple-element.205), channel_id=1, source_target_pairs={{8,0},{16,8},{24,16},{9,1},{17,9},{25,17},{10,2},{18,10},{26,18},{... | collective-permute-start | bytes 393224 | tf_op jit(solution)/shard_map/ppermute | solution.py:22
  132.5 5.9 %pad_maximum_fusion = (bf16[2,64,72,132]{3,1,2,0:T(8,128)(2,1)S(1)}, bf16[2,64,72,132]{3,1,2,0:T(8,128)(2,1)S(1)}) fusion(bf16[2,64,72,4]{3,1,2,0:T(8,128)(2,1)} %copy.77, bf16[2,64,4,128]{3,1,2,0:T(8,128)(2,1)S(1)} %collective-permute-done.12, bf16[2,64,64,128]{3,1,2,0:T(8,128)(2,1)S(1)} %copy-done.1, ...), kind=kLoop, calls=%fused_computation.25 | loop fusion | flops 19464192 | bytes 7372800 | tf_op jit(solution)/shard_map/concatenate | solution.py:23
  154.4 15.0 %fusion.5 = (f32[2,64,128]{2,1,0:T(8,128)S(1)}, bf16[2,64,64,128]{3,1,2,0:T(8,128)(2,1)}) fusion(bf16[2,64,72,132]{3,1,2,0:T(8,128)(2,1)} %copy-done.9, bf16[9,64,64]{2,1,0:T(8,128)(2,1)S(1)} %copy-done.14, f32[2,64,128,64]{2,3,1,0:T(8,128)} %fusion.28, f32[2,64,128,64]{2,3,1,0:T(8,128)} %fusion.30, f32[2,64,128,64]{2,3,1,0:T(8,128)} %fusion.32, ...), kind=kOutput, calls=%fused_computation.26 | convolution fusion | flops 148881408 | bytes 39927808 | tf_op jit(solution)/shard_map/oc,nchw->nohw/dot_general | solution.py:40
  173.3 6.6 %all-to-all-start = ((bf16[2,64,64,128]{3,1,0,2:T(8,128)(2,1)}), bf16[2,64,64,128]{3,1,0,2:T(8,128)(2,1)S(1)}, u32[]{:S(2)}, u32[]{:S(2)}) async-start(bf16[2,64,64,128]{3,1,0,2:T(8,128)(2,1)} %copy.78), calls=%async_computation | async-start | bytes 4194304 | tf_op jit(solution)/shard_map/all_to_all | solution.py:91
  180.4 37.8 %collective-permute-done = s32[2,8,1]{1,2,0:T(1,128)S(1)} collective-permute-done((s32[2,8,1]{1,2,0:T(1,128)S(1)}, s32[2,8,1]{1,2,0:T(1,128)S(1)}, u32[]{:S(2)}, u32[]{:S(2)}) %collective-permute-start) | collective-permute-done | bytes 96 | tf_op jit(solution)/shard_map/ppermute | solution.py:94
  218.2 4.8 collective-permute-done.1
  223.0 4.8 collective-permute-done.2
  251.3 204.0 %while.18 = (s32[]{:T(128)}, f32[64,128]{1,0:T(8,128)S(1)}, f32[64,128]{1,0:T(8,128)S(1)}, f32[64,64,128]{2,0,1:T(8,128)}, s32[64]{0:T(128)S(1)}, /*index=5*/s32...) while((s32[]{:T(128)}, f32[64,128]{1,0:T(8,128)S(1)}, ...), condition=%wide.region_4.5_spmd.clone, body=%wide.region_1.4_spmd.clone.sunk | while | flops 280019072 | bytes 33031948 | solution.py:118
  253.1 5.1 %fusion.117 = (f32[64,128]{1,0:T(8,128)S(1)}, f32[64,128]{1,0:T(8,128)S(1)}, bf16[64,128,128]{1,2,0:T(8,128)(2,1)}) fusion(f32[128,128]{0,1:T(8,128)S(1)} %get-tuple-element.268, bf16[64,64,128]{2,0,1:T(8,128)(2,1)} %get-tuple-element.308, bf16[64,64,128]{2,1,0:T(8,128)(2,1)S(1)} %reshape.96, s32[64]{0:T(128)S(1)} %get-tuple-element.306, ...), kind=kOutput, calls=%fused_computation.2.clone.1 | convolution fusion | flops 144687104 | bytes 4391424 | tf_op jit(solution)/shard_map/while/body/eval_jaxpr/cri,crm->rim/dot_general | solution.py:59
  264.5 5.1 %fusion.117 = (f32[64,128]{1,0:T(8,128)S(1)}, f32[64,128]{1,0:T(8,128)S(1)}, bf16[64,128,128]{1,2,0:T(8,128)(2,1)}) fusion(f32[128,128]{0,1:T(8,128)S(1)} %get-tuple-element.268, bf16[64,64,128]{2,0,1:T(8,128)(2,1)} %get-tuple-element.308, bf16[64,64,128]{2,1,0:T(8,128)(2,1)S(1)} %reshape.96, s32[64]{0:T(128)S(1)} %get-tuple-element.306, ...), kind=kOutput, calls=%fused_computation.2.clone.1 | convolution fusion | flops 144687104 | bytes 4391424 | tf_op jit(solution)/shard_map/while/body/eval_jaxpr/cri,crm->rim/dot_general | solution.py:59
  275.8 5.1 %fusion.117 = (f32[64,128]{1,0:T(8,128)S(1)}, f32[64,128]{1,0:T(8,128)S(1)}, bf16[64,128,128]{1,2,0:T(8,128)(2,1)}) fusion(f32[128,128]{0,1:T(8,128)S(1)} %get-tuple-element.268, bf16[64,64,128]{2,0,1:T(8,128)(2,1)} %get-tuple-element.308, bf16[64,64,128]{2,1,0:T(8,128)(2,1)S(1)} %reshape.96, s32[64]{0:T(128)S(1)} %get-tuple-element.306, ...), kind=kOutput, calls=%fused_computation.2.clone.1 | convolution fusion | flops 144687104 | bytes 4391424 | tf_op jit(solution)/shard_map/while/body/eval_jaxpr/cri,crm->rim/dot_general | solution.py:59
  287.1 5.1 %fusion.117 = (f32[64,128]{1,0:T(8,128)S(1)}, f32[64,128]{1,0:T(8,128)S(1)}, bf16[64,128,128]{1,2,0:T(8,128)(2,1)}) fusion(f32[128,128]{0,1:T(8,128)S(1)} %get-tuple-element.268, bf16[64,64,128]{2,0,1:T(8,128)(2,1)} %get-tuple-element.308, bf16[64,64,128]{2,1,0:T(8,128)(2,1)S(1)} %reshape.96, s32[64]{0:T(128)S(1)} %get-tuple-element.306, ...), kind=kOutput, calls=%fused_computation.2.clone.1 | convolution fusion | flops 144687104 | bytes 4391424 | tf_op jit(solution)/shard_map/while/body/eval_jaxpr/cri,crm->rim/dot_general | solution.py:59
  298.5 5.1 %fusion.117 = (f32[64,128]{1,0:T(8,128)S(1)}, f32[64,128]{1,0:T(8,128)S(1)}, bf16[64,128,128]{1,2,0:T(8,128)(2,1)}) fusion(f32[128,128]{0,1:T(8,128)S(1)} %get-tuple-element.268, bf16[64,64,128]{2,0,1:T(8,128)(2,1)} %get-tuple-element.308, bf16[64,64,128]{2,1,0:T(8,128)(2,1)S(1)} %reshape.96, s32[64]{0:T(128)S(1)} %get-tuple-element.306, ...), kind=kOutput, calls=%fused_computation.2.clone.1 | convolution fusion | flops 144687104 | bytes 4391424 | tf_op jit(solution)/shard_map/while/body/eval_jaxpr/cri,crm->rim/dot_general | solution.py:59
  309.8 5.1 %fusion.117 = (f32[64,128]{1,0:T(8,128)S(1)}, f32[64,128]{1,0:T(8,128)S(1)}, bf16[64,128,128]{1,2,0:T(8,128)(2,1)}) fusion(f32[128,128]{0,1:T(8,128)S(1)} %get-tuple-element.268, bf16[64,64,128]{2,0,1:T(8,128)(2,1)} %get-tuple-element.308, bf16[64,64,128]{2,1,0:T(8,128)(2,1)S(1)} %reshape.96, s32[64]{0:T(128)S(1)} %get-tuple-element.306, ...), kind=kOutput, calls=%fused_computation.2.clone.1 | convolution fusion | flops 144687104 | bytes 4391424 | tf_op jit(solution)/shard_map/while/body/eval_jaxpr/cri,crm->rim/dot_general | solution.py:59
  321.1 5.1 %fusion.117 = (f32[64,128]{1,0:T(8,128)S(1)}, f32[64,128]{1,0:T(8,128)S(1)}, bf16[64,128,128]{1,2,0:T(8,128)(2,1)}) fusion(f32[128,128]{0,1:T(8,128)S(1)} %get-tuple-element.268, bf16[64,64,128]{2,0,1:T(8,128)(2,1)} %get-tuple-element.308, bf16[64,64,128]{2,1,0:T(8,128)(2,1)S(1)} %reshape.96, s32[64]{0:T(128)S(1)} %get-tuple-element.306, ...), kind=kOutput, calls=%fused_computation.2.clone.1 | convolution fusion | flops 144687104 | bytes 4391424 | tf_op jit(solution)/shard_map/while/body/eval_jaxpr/cri,crm->rim/dot_general | solution.py:59
  332.5 5.1 %fusion.117 = (f32[64,128]{1,0:T(8,128)S(1)}, f32[64,128]{1,0:T(8,128)S(1)}, bf16[64,128,128]{1,2,0:T(8,128)(2,1)}) fusion(f32[128,128]{0,1:T(8,128)S(1)} %get-tuple-element.268, bf16[64,64,128]{2,0,1:T(8,128)(2,1)} %get-tuple-element.308, bf16[64,64,128]{2,1,0:T(8,128)(2,1)S(1)} %reshape.96, s32[64]{0:T(128)S(1)} %get-tuple-element.306, ...), kind=kOutput, calls=%fused_computation.2.clone.1 | convolution fusion | flops 144687104 | bytes 4391424 | tf_op jit(solution)/shard_map/while/body/eval_jaxpr/cri,crm->rim/dot_general | solution.py:59
  343.8 5.1 %fusion.117 = (f32[64,128]{1,0:T(8,128)S(1)}, f32[64,128]{1,0:T(8,128)S(1)}, bf16[64,128,128]{1,2,0:T(8,128)(2,1)}) fusion(f32[128,128]{0,1:T(8,128)S(1)} %get-tuple-element.268, bf16[64,64,128]{2,0,1:T(8,128)(2,1)} %get-tuple-element.308, bf16[64,64,128]{2,1,0:T(8,128)(2,1)S(1)} %reshape.96, s32[64]{0:T(128)S(1)} %get-tuple-element.306, ...), kind=kOutput, calls=%fused_computation.2.clone.1 | convolution fusion | flops 144687104 | bytes 4391424 | tf_op jit(solution)/shard_map/while/body/eval_jaxpr/cri,crm->rim/dot_general | solution.py:59
  355.1 5.1 %fusion.117 = (f32[64,128]{1,0:T(8,128)S(1)}, f32[64,128]{1,0:T(8,128)S(1)}, bf16[64,128,128]{1,2,0:T(8,128)(2,1)}) fusion(f32[128,128]{0,1:T(8,128)S(1)} %get-tuple-element.268, bf16[64,64,128]{2,0,1:T(8,128)(2,1)} %get-tuple-element.308, bf16[64,64,128]{2,1,0:T(8,128)(2,1)S(1)} %reshape.96, s32[64]{0:T(128)S(1)} %get-tuple-element.306, ...), kind=kOutput, calls=%fused_computation.2.clone.1 | convolution fusion | flops 144687104 | bytes 4391424 | tf_op jit(solution)/shard_map/while/body/eval_jaxpr/cri,crm->rim/dot_general | solution.py:59
  366.5 5.1 %fusion.117 = (f32[64,128]{1,0:T(8,128)S(1)}, f32[64,128]{1,0:T(8,128)S(1)}, bf16[64,128,128]{1,2,0:T(8,128)(2,1)}) fusion(f32[128,128]{0,1:T(8,128)S(1)} %get-tuple-element.268, bf16[64,64,128]{2,0,1:T(8,128)(2,1)} %get-tuple-element.308, bf16[64,64,128]{2,1,0:T(8,128)(2,1)S(1)} %reshape.96, s32[64]{0:T(128)S(1)} %get-tuple-element.306, ...), kind=kOutput, calls=%fused_computation.2.clone.1 | convolution fusion | flops 144687104 | bytes 4391424 | tf_op jit(solution)/shard_map/while/body/eval_jaxpr/cri,crm->rim/dot_general | solution.py:59
  377.8 5.1 %fusion.117 = (f32[64,128]{1,0:T(8,128)S(1)}, f32[64,128]{1,0:T(8,128)S(1)}, bf16[64,128,128]{1,2,0:T(8,128)(2,1)}) fusion(f32[128,128]{0,1:T(8,128)S(1)} %get-tuple-element.268, bf16[64,64,128]{2,0,1:T(8,128)(2,1)} %get-tuple-element.308, bf16[64,64,128]{2,1,0:T(8,128)(2,1)S(1)} %reshape.96, s32[64]{0:T(128)S(1)} %get-tuple-element.306, ...), kind=kOutput, calls=%fused_computation.2.clone.1 | convolution fusion | flops 144687104 | bytes 4391424 | tf_op jit(solution)/shard_map/while/body/eval_jaxpr/cri,crm->rim/dot_general | solution.py:59
  389.2 5.1 %fusion.117 = (f32[64,128]{1,0:T(8,128)S(1)}, f32[64,128]{1,0:T(8,128)S(1)}, bf16[64,128,128]{1,2,0:T(8,128)(2,1)}) fusion(f32[128,128]{0,1:T(8,128)S(1)} %get-tuple-element.268, bf16[64,64,128]{2,0,1:T(8,128)(2,1)} %get-tuple-element.308, bf16[64,64,128]{2,1,0:T(8,128)(2,1)S(1)} %reshape.96, s32[64]{0:T(128)S(1)} %get-tuple-element.306, ...), kind=kOutput, calls=%fused_computation.2.clone.1 | convolution fusion | flops 144687104 | bytes 4391424 | tf_op jit(solution)/shard_map/while/body/eval_jaxpr/cri,crm->rim/dot_general | solution.py:59
  400.5 5.1 %fusion.117 = (f32[64,128]{1,0:T(8,128)S(1)}, f32[64,128]{1,0:T(8,128)S(1)}, bf16[64,128,128]{1,2,0:T(8,128)(2,1)}) fusion(f32[128,128]{0,1:T(8,128)S(1)} %get-tuple-element.268, bf16[64,64,128]{2,0,1:T(8,128)(2,1)} %get-tuple-element.308, bf16[64,64,128]{2,1,0:T(8,128)(2,1)S(1)} %reshape.96, s32[64]{0:T(128)S(1)} %get-tuple-element.306, ...), kind=kOutput, calls=%fused_computation.2.clone.1 | convolution fusion | flops 144687104 | bytes 4391424 | tf_op jit(solution)/shard_map/while/body/eval_jaxpr/cri,crm->rim/dot_general | solution.py:59
  411.8 5.1 %fusion.117 = (f32[64,128]{1,0:T(8,128)S(1)}, f32[64,128]{1,0:T(8,128)S(1)}, bf16[64,128,128]{1,2,0:T(8,128)(2,1)}) fusion(f32[128,128]{0,1:T(8,128)S(1)} %get-tuple-element.268, bf16[64,64,128]{2,0,1:T(8,128)(2,1)} %get-tuple-element.308, bf16[64,64,128]{2,1,0:T(8,128)(2,1)S(1)} %reshape.96, s32[64]{0:T(128)S(1)} %get-tuple-element.306, ...), kind=kOutput, calls=%fused_computation.2.clone.1 | convolution fusion | flops 144687104 | bytes 4391424 | tf_op jit(solution)/shard_map/while/body/eval_jaxpr/cri,crm->rim/dot_general | solution.py:59
  423.2 5.1 %fusion.117 = (f32[64,128]{1,0:T(8,128)S(1)}, f32[64,128]{1,0:T(8,128)S(1)}, bf16[64,128,128]{1,2,0:T(8,128)(2,1)}) fusion(f32[128,128]{0,1:T(8,128)S(1)} %get-tuple-element.268, bf16[64,64,128]{2,0,1:T(8,128)(2,1)} %get-tuple-element.308, bf16[64,64,128]{2,1,0:T(8,128)(2,1)S(1)} %reshape.96, s32[64]{0:T(128)S(1)} %get-tuple-element.306, ...), kind=kOutput, calls=%fused_computation.2.clone.1 | convolution fusion | flops 144687104 | bytes 4391424 | tf_op jit(solution)/shard_map/while/body/eval_jaxpr/cri,crm->rim/dot_general | solution.py:59
  434.5 5.1 %fusion.117 = (f32[64,128]{1,0:T(8,128)S(1)}, f32[64,128]{1,0:T(8,128)S(1)}, bf16[64,128,128]{1,2,0:T(8,128)(2,1)}) fusion(f32[128,128]{0,1:T(8,128)S(1)} %get-tuple-element.268, bf16[64,64,128]{2,0,1:T(8,128)(2,1)} %get-tuple-element.308, bf16[64,64,128]{2,1,0:T(8,128)(2,1)S(1)} %reshape.96, s32[64]{0:T(128)S(1)} %get-tuple-element.306, ...), kind=kOutput, calls=%fused_computation.2.clone.1 | convolution fusion | flops 144687104 | bytes 4391424 | tf_op jit(solution)/shard_map/while/body/eval_jaxpr/cri,crm->rim/dot_general | solution.py:59
  445.8 5.1 %fusion.117 = (f32[64,128]{1,0:T(8,128)S(1)}, f32[64,128]{1,0:T(8,128)S(1)}, bf16[64,128,128]{1,2,0:T(8,128)(2,1)}) fusion(f32[128,128]{0,1:T(8,128)S(1)} %get-tuple-element.268, bf16[64,64,128]{2,0,1:T(8,128)(2,1)} %get-tuple-element.308, bf16[64,64,128]{2,1,0:T(8,128)(2,1)S(1)} %reshape.96, s32[64]{0:T(128)S(1)} %get-tuple-element.306, ...), kind=kOutput, calls=%fused_computation.2.clone.1 | convolution fusion | flops 144687104 | bytes 4391424 | tf_op jit(solution)/shard_map/while/body/eval_jaxpr/cri,crm->rim/dot_general | solution.py:59
  467.3 5.0 all-to-all-start.1
  472.3 26.6 %all-to-all-done.1 = bf16[8,2,32768]{2,1,0:T(2,128)(2,1)S(1)} async-done(((bf16[8,2,32768]{2,1,0:T(2,128)(2,1)}), bf16[8,2,32768]{2,1,0:T(2,128)(2,1)S(1)}, u32[]{:S(2)}, u32[]{:S(2)}) %all-to-all-start.1) | async-done | bytes 1048608 | tf_op jit(solution)/shard_map/all_to_all | solution.py:127
  (294 shorter events, 258.7 us)
Async XLA Ops:
  0.6 9.9 %copy-start.7 = (bf16[2,64,64,128]{3,2,1,0:T(8,128)(2,1)S(1)}, bf16[2,64,64,128]{3,2,1,0:T(8,128)(2,1)}, u32[]{:S(2)}) copy-start(bf16[2,64,64,128]{3,2,1,0:T(8,128)(2,1)} %param.6) | copy-start | bytes 6291460
  0.6 9.9 %copy-start.13 = (bf16[9,64,64]{2,1,0:T(8,128)(2,1)S(1)}, bf16[9,64,64]{2,1,0:T(8,128)(2,1)}, u32[]{:S(2)}) copy-start(bf16[9,64,64]{2,1,0:T(8,128)(2,1)} %param.7) | copy-start | bytes 221188
  3.7 12.0 %copy-start.10 = (bf16[2,64,64,128]{3,1,2,0:T(8,128)(2,1)}, bf16[2,64,64,128]{3,1,2,0:T(8,128)(2,1)S(1)}, u32[]{:S(2)}) copy-start(bf16[2,64,64,128]{3,1,2,0:T(8,128)(2,1)S(1)} %copy.63) | copy-start | bytes 6291460
  3.8 10.5 %collective-permute-start.7 = (bf16[2,64,2,128]{3,1,2,0:T(8,128)(2,1)S(1)}, bf16[2,64,2,128]{3,1,2,0:T(8,128)(2,1)S(1)}, u32[]{:S(2)}, u32[]{:S(2)}) collective-permute-start(bf16[2,64,2,128]{3,1,2,0:T(8,128)(2,1)S(1)} %get-tuple-element.206), channel_id=1, source_target_pairs={{0,8},{8,16},{16,24},{1,9},{9,17},{17,25},{2,10},{10,18},{18,26},{... | collective-permute-start | bytes 196616 | tf_op jit(solution)/shard_map/ppermute | solution.py:19
  7.2 8.6 %collective-permute-start.8 = (bf16[2,64,2,128]{3,1,2,0:T(8,128)(2,1)S(1)}, bf16[2,64,2,128]{3,1,2,0:T(8,128)(2,1)S(1)}, u32[]{:S(2)}, u32[]{:S(2)}) collective-permute-start(bf16[2,64,2,128]{3,1,2,0:T(8,128)(2,1)S(1)} %get-tuple-element.207), channel_id=1, source_target_pairs={{8,0},{16,8},{24,16},{9,1},{17,9},{25,17},{10,2},{18,10},{26,18},{... | collective-permute-start | bytes 196616 | tf_op jit(solution)/shard_map/ppermute | solution.py:22
  22.7 28.0 %collective-permute-start.10 = (bf16[2,64,68,2]{2,1,3,0:T(8,128)(2,1)S(1)}, bf16[2,64,68,2]{2,1,3,0:T(8,128)(2,1)S(1)}, u32[]{:S(2)}, u32[]{:S(2)}) collective-permute-start(bf16[2,64,68,2]{2,1,3,0:T(8,128)(2,1)S(1)} %copy.70), channel_id=1, source_target_pairs={{1,0},{2,1},{3,2},{4,3},{5,4},{6,5},{7,6},{9,8},{10,9},{11,10},{12... | collective-permute-start | bytes 104456 | tf_op jit(solution)/shard_map/ppermute | solution.py:22
  27.7 7.5 %copy-start.11 = (bf16[2,64,64,128]{3,1,2,0:T(8,128)(2,1)S(1)}, bf16[2,64,64,128]{3,1,2,0:T(8,128)(2,1)}, u32[]{:S(2)}) copy-start(bf16[2,64,64,128]{3,1,2,0:T(8,128)(2,1)} %copy-done.10) | copy-start | bytes 6291460
  27.7 10.2 %collective-permute-start.9 = (bf16[2,64,68,2]{2,1,3,0:T(8,128)(2,1)S(1)}, bf16[2,64,68,2]{2,1,3,0:T(8,128)(2,1)S(1)}, u32[]{:S(2)}, u32[]{:S(2)}) collective-permute-start(bf16[2,64,68,2]{2,1,3,0:T(8,128)(2,1)S(1)} %copy.67), channel_id=1, source_target_pairs={{0,1},{1,2},{2,3},{3,4},{4,5},{5,6},{6,7},{8,9},{9,10},{10,11},{11... | collective-permute-start | bytes 104456 | tf_op jit(solution)/shard_map/ppermute | solution.py:19
  55.2 5.3 %copy-start.4 = (bf16[2,64,68,2]{3,1,2,0:T(8,128)(2,1)S(1)}, bf16[2,64,68,2]{3,1,2,0:T(8,128)(2,1)}, u32[]{:S(2)}) copy-start(bf16[2,64,68,2]{3,1,2,0:T(8,128)(2,1)} %copy.71) | copy-start | bytes 104452
  67.2 31.9 %copy-start.14 = (bf16[9,64,64]{2,1,0:T(8,128)(2,1)S(1)}, bf16[9,64,64]{2,1,0:T(8,128)(2,1)}, u32[]{:S(2)}) copy-start(bf16[9,64,64]{2,1,0:T(8,128)(2,1)} %param.8) | copy-start | bytes 221188
  79.7 22.4 %copy-start = (bf16[2,64,64,128]{3,1,2,0:T(8,128)(2,1)}, bf16[2,64,64,128]{3,1,2,0:T(8,128)(2,1)S(1)}, u32[]{:S(2)}) copy-start(bf16[2,64,64,128]{3,1,2,0:T(8,128)(2,1)S(1)} %fusion.11) | copy-start | bytes 6291460
  79.8 22.1 %collective-permute-start.11 = (bf16[2,64,4,128]{3,1,2,0:T(8,128)(2,1)S(1)}, bf16[2,64,4,128]{3,1,2,0:T(8,128)(2,1)S(1)}, u32[]{:S(2)}, u32[]{:S(2)}) collective-permute-start(bf16[2,64,4,128]{3,1,2,0:T(8,128)(2,1)S(1)} %get-tuple-element.204), channel_id=1, source_target_pairs={{0,8},{8,16},{16,24},{1,9},{9,17},{17,25},{2,10},{10,18},{18,26},{... | collective-permute-start | bytes 393224 | tf_op jit(solution)/shard_map/ppermute | solution.py:19
  82.3 19.6 %collective-permute-start.12 = (bf16[2,64,4,128]{3,1,2,0:T(8,128)(2,1)S(1)}, bf16[2,64,4,128]{3,1,2,0:T(8,128)(2,1)S(1)}, u32[]{:S(2)}, u32[]{:S(2)}) collective-permute-start(bf16[2,64,4,128]{3,1,2,0:T(8,128)(2,1)S(1)} %get-tuple-element.205), channel_id=1, source_target_pairs={{8,0},{16,8},{24,16},{9,1},{17,9},{25,17},{10,2},{18,10},{26,18},{... | collective-permute-start | bytes 393224 | tf_op jit(solution)/shard_map/ppermute | solution.py:22
  105.5 12.1 %copy-start.1 = (bf16[2,64,64,128]{3,1,2,0:T(8,128)(2,1)S(1)}, bf16[2,64,64,128]{3,1,2,0:T(8,128)(2,1)}, u32[]{:S(2)}) copy-start(bf16[2,64,64,128]{3,1,2,0:T(8,128)(2,1)} %copy-done) | copy-start | bytes 6291460
  109.7 13.3 %collective-permute-start.13 = (bf16[2,64,72,4]{2,1,3,0:T(8,128)(2,1)S(1)}, bf16[2,64,72,4]{2,1,3,0:T(8,128)(2,1)S(1)}, u32[]{:S(2)}, u32[]{:S(2)}) collective-permute-start(bf16[2,64,72,4]{2,1,3,0:T(8,128)(2,1)S(1)} %copy.74), channel_id=1, source_target_pairs={{0,1},{1,2},{2,3},{3,4},{4,5},{5,6},{6,7},{8,9},{9,10},{10,11},{11... | collective-permute-start | bytes 221192 | tf_op jit(solution)/shard_map/ppermute | solution.py:19
  116.3 11.4 %collective-permute-start.14 = (bf16[2,64,72,4]{2,1,3,0:T(8,128)(2,1)S(1)}, bf16[2,64,72,4]{2,1,3,0:T(8,128)(2,1)S(1)}, u32[]{:S(2)}, u32[]{:S(2)}) collective-permute-start(bf16[2,64,72,4]{2,1,3,0:T(8,128)(2,1)S(1)} %copy.76), channel_id=1, source_target_pairs={{1,0},{2,1},{3,2},{4,3},{5,4},{6,5},{7,6},{9,8},{10,9},{11,10},{12... | collective-permute-start | bytes 221192 | tf_op jit(solution)/shard_map/ppermute | solution.py:22
  138.4 8.9 %copy-start.9 = (bf16[2,64,72,132]{3,1,2,0:T(8,128)(2,1)}, bf16[2,64,72,132]{3,1,2,0:T(8,128)(2,1)S(1)}, u32[]{:S(2)}) copy-start(bf16[2,64,72,132]{3,1,2,0:T(8,128)(2,1)S(1)} %get-tuple-element.196) | copy-start | bytes 7299076
  171.7 8.2 %copy-start.15 = (s32[2,8,1]{1,2,0:T(1,128)S(1)}, s32[2,8,1]{1,2,0:T(1,128)}, u32[]{:S(2)}) copy-start(s32[2,8,1]{1,2,0:T(1,128)} %param.9) | copy-start | bytes 196
  173.3 74.2 %all-to-all-start = ((bf16[2,64,64,128]{3,1,0,2:T(8,128)(2,1)}), bf16[2,64,64,128]{3,1,0,2:T(8,128)(2,1)S(1)}, u32[]{:S(2)}, u32[]{:S(2)}) async-start(bf16[2,64,64,128]{3,1,0,2:T(8,128)(2,1)} %copy.78), calls=%async_computation | async-start | bytes 4194304 | tf_op jit(solution)/shard_map/all_to_all | solution.py:91
  179.9 38.3 %collective-permute-start = (s32[2,8,1]{1,2,0:T(1,128)S(1)}, s32[2,8,1]{1,2,0:T(1,128)S(1)}, u32[]{:S(2)}, u32[]{:S(2)}) collective-permute-start(s32[2,8,1]{1,2,0:T(1,128)S(1)} %copy-done.15), channel_id=1, source_target_pairs={{0,1},{1,2},{2,3},{3,4},{4,5},{5,6},{6,7},{7,0},{8,9},{9,10},{10,1... | collective-permute-start | bytes 200 | tf_op jit(solution)/shard_map/ppermute | solution.py:94
  218.2 4.8 collective-permute-start.1
  223.0 4.8 collective-permute-start.2
  227.8 4.8 collective-permute-start.3
  232.6 4.8 collective-permute-start.4
  237.4 4.8 collective-permute-start.5
  242.2 5.0 collective-permute-start.6
  253.1 5.1 %copy-start.2 = (f32[64,64,128]{2,0,1:T(8,128)S(1)}, f32[64,64,128]{2,0,1:T(8,128)}, u32[]{:S(2)}) copy-start(f32[64,64,128]{2,0,1:T(8,128)} %get-tuple-element.291) | copy-start | bytes 6291460 | tf_op jit(solution)/shard_map/while
  275.8 5.1 %copy-start.2 = (f32[64,64,128]{2,0,1:T(8,128)S(1)}, f32[64,64,128]{2,0,1:T(8,128)}, u32[]{:S(2)}) copy-start(f32[64,64,128]{2,0,1:T(8,128)} %get-tuple-element.291) | copy-start | bytes 6291460 | tf_op jit(solution)/shard_map/while
  287.1 5.1 %copy-start.2 = (f32[64,64,128]{2,0,1:T(8,128)S(1)}, f32[64,64,128]{2,0,1:T(8,128)}, u32[]{:S(2)}) copy-start(f32[64,64,128]{2,0,1:T(8,128)} %get-tuple-element.291) | copy-start | bytes 6291460 | tf_op jit(solution)/shard_map/while
  298.5 5.1 %copy-start.2 = (f32[64,64,128]{2,0,1:T(8,128)S(1)}, f32[64,64,128]{2,0,1:T(8,128)}, u32[]{:S(2)}) copy-start(f32[64,64,128]{2,0,1:T(8,128)} %get-tuple-element.291) | copy-start | bytes 6291460 | tf_op jit(solution)/shard_map/while
  456.0 11.3 %all-to-all-start.2 = ((f32[8,8,128]{2,0,1:T(8,128)}), f32[8,8,128]{2,0,1:T(8,128)S(1)}, u32[]{:S(2)}, u32[]{:S(2)}) async-start(f32[8,8,128]{2,0,1:T(8,128)} %copy.84), calls=%async_computation.2 | async-start | bytes 65536 | tf_op jit(solution)/shard_map/all_to_all | solution.py:128
  467.3 31.6 %all-to-all-start.1 = ((bf16[8,2,32768]{2,1,0:T(2,128)(2,1)}), bf16[8,2,32768]{2,1,0:T(2,128)(2,1)S(1)}, u32[]{:S(2)}, u32[]{:S(2)}) async-start(bf16[8,2,32768]{2,1,0:T(2,128)(2,1)} %reshape.93), calls=%async_computation.1 | async-start | bytes 2097152 | tf_op jit(solution)/shard_map/all_to_all | solution.py:127
  (36 other events, 111.6 us)
